TPU v7x, 256 devices: a whole 4x4x8 slice. The times are simulated.
256 devices in a mesh: chan: 32 (over z, y), sky: 8 (over x, core).
Axes of the slice: x: 4, y: 4, z: 8, core: 2. Of those that a mesh axis runs over, the one named last changes fastest.
Arguments:
- sky_map: float32 [1024, 131072], P('chan', 'sky')
- templates: float32 [1024, 30], replicated, may hold values from -6 to 6
- noise_var: float32 [1024], replicated, may hold values from 0.5 to 2
- block_order: int32 [8, 128], P('sky'), may hold values from 0 to 127, each once within a row
- patch_count: int32 [8, 32], P('sky'), may hold values from 1 to 8, as said below
- slab_dest: int32 [8, 32, 8], P('sky'), may hold values from 0 to 7, as said below
Outputs:
- slab_cube: float32 [1024, 2048, 128], P('chan', 'sky')
Inputs may be any that keep to these rules, and one draw needn't show every extreme that they name: `slab_dest`: taken in order of owners and then slots, the live slots of a sky group (slots below the owner's count) cycle through all 8 slabs in one fixed order, so every slab gets exactly 16 live slots of each group and no owner names a slab more than 1 times; slots at or beyond the owner's count are ignored. `patch_count`: in each sky group the counts sum to 128 and the largest is 8. `block_order`: each row is an ordering of the group's 128 blocks.
All inputs are finite; a program needn't handle non-finite values.
Results may differ from a plain program's by a relative error of at most 0.0003.
Values sent between devices are 32-bit elements; how exact they have to be, the bound alone decides.
A program may use at most 64 MiB of HBM per device.

v0:
```python
import jax
import jax.numpy as jnp
from jax import lax
from jax.sharding import PartitionSpec as P

NU = 1024
BLK = 128
CAP = 8


def owner_blocks(order_row, counts_row):
    offsets = jnp.cumsum(counts_row) - counts_row
    slot_index = jnp.arange(CAP, dtype=jnp.int32)
    live_slots = slot_index[None, :] < counts_row[:, None]
    position = jnp.where(live_slots, offsets[:, None] + slot_index[None, :], 0)
    return (jnp.take(order_row, position, axis=0), live_slots)


def slab_sources(dest_row, block_count, sky_count, slab_cap):
    slot_index = jnp.arange(dest_row.shape[0], dtype=jnp.int32)
    live_slots = slot_index < block_count
    earlier = (
        (dest_row[:, None] == dest_row[None, :])
        & live_slots[:, None]
        & live_slots[None, :]
        & (slot_index[None, :] < slot_index[:, None])
    )
    rank_in_slab = jnp.sum(earlier.astype(jnp.int32), axis=1)
    target_row = dest_row * slab_cap + rank_in_slab
    row_index = jnp.arange(sky_count * slab_cap, dtype=jnp.int32)
    matches = (target_row[None, :] == row_index[:, None]) & live_slots[None, :]
    source_slot = jnp.sum(jnp.where(matches, slot_index[None, :], 0), axis=1)
    return (source_slot, jnp.any(matches, axis=1))


def template_amplitudes(pixels, block_count, templates, noise_var):
    highest = lax.Precision.HIGHEST
    covariance = jnp.dot(pixels, pixels.T, precision=highest) / (block_count * BLK).astype(
        jnp.float32
    ) + jnp.diag(noise_var)
    factor = jnp.linalg.cholesky(covariance)
    weighted = jax.scipy.linalg.cho_solve((factor, True), templates)
    gram_matrix = jnp.dot(templates.T, weighted, precision=highest)
    projected = jnp.dot(weighted.T, pixels, precision=highest)
    return jax.scipy.linalg.cho_solve((jnp.linalg.cholesky(gram_matrix), True), projected)


def on_device(sky_map, templates, noise_var, block_order, patch_count, slab_dest):
    chan_count = lax.axis_size("chan")
    sky_count = lax.axis_size("sky")
    member = lax.axis_index("chan")
    chan_rows = sky_map.shape[0]
    slab_cap = (CAP + sky_count - 1) // sky_count
    local_map = sky_map.reshape(chan_rows, -1, BLK)
    blocks, live_slots = owner_blocks(block_order[0], patch_count[0])
    outgoing = jnp.take(local_map, blocks.reshape(-1), axis=1).reshape(
        chan_rows, chan_count, CAP, BLK
    )
    outgoing = jnp.where(live_slots[None, :, :, None], outgoing, 0.0).reshape(
        chan_rows, chan_count, CAP * BLK
    )
    pixels = lax.all_to_all(outgoing, "chan", split_axis=1, concat_axis=0, tiled=True).reshape(
        NU, CAP * BLK
    )
    block_count = lax.dynamic_index_in_dim(patch_count[0], member, 0, keepdims=False)
    amplitudes = template_amplitudes(pixels, block_count, templates, noise_var)
    cleaned = pixels - jnp.dot(templates, amplitudes, precision=lax.Precision.HIGHEST)
    own_dest = lax.dynamic_index_in_dim(slab_dest[0], member, 0, keepdims=False)
    source_slot, filled = slab_sources(own_dest, block_count, sky_count, slab_cap)
    buffer = jnp.take(cleaned.reshape(NU, CAP, BLK), source_slot, axis=1)
    buffer = jnp.where(filled[None, :, None], buffer, 0.0).reshape(NU, sky_count, slab_cap, BLK)
    arrived = lax.all_to_all(
        lax.all_to_all(buffer, "chan", split_axis=0, concat_axis=2, tiled=True),
        "sky",
        split_axis=1,
        concat_axis=1,
        tiled=True,
    )
    return arrived.reshape(chan_rows, -1, BLK)


def solution(mesh):
    return jax.shard_map(
        on_device,
        mesh=mesh,
        in_specs=(P("chan", "sky"), P(), P(), P("sky", None), P("sky", None), P("sky", None, None)),
        out_specs=P("chan", "sky", None),
        check_vma=False,
    )
```

profile of v0, /device:TPU:24, one launch (start us, length us, event | category | flops | bytes accessed | tf_op | source)
XLA Modules:
  0.0 702.6 jit_solution(13540697992947009)
XLA Ops:
  6.7 1.6 copy_bitcast_fusion
  8.3 1.9 gather_fusion
  10.3 3.1 gather_fusion.1
  13.4 6.5 copy.40
  19.9 4.9 gather.27
  25.2 2.7 select_select_fusion.1
  27.9 4.4 copy.41
  32.4 12.2 %all-to-all-start = ((f32[32,32,1024]{2,0,1:T(8,128)}), f32[32,32,1024]{2,0,1:T(8,128)}, u32[]{:S(2)}, u32[]{:S(2)}) async-start(f32[32,32,1024]{2,0,1:T(8,128)} %copy.41), calls=%async_computation | async-start | bytes 8388608 | tf_op jit(solution)/shard_map/all_to_all | solution.py:62
  45.4 94.8 %all-to-all-done = f32[32,32,1024]{2,0,1:T(8,128)} async-done(((f32[32,32,1024]{2,0,1:T(8,128)}), f32[32,32,1024]{2,0,1:T(8,128)}, u32[]{:S(2)}, u32[]{:S(2)}) %all-to-all-start) | async-done | bytes 4194336 | tf_op jit(solution)/shard_map/all_to_all | solution.py:62
  140.2 18.1 %broadcast_divide_fusion = f32[1024,1024]{1,0:T(8,128)} fusion(f32[]{:T(128)S(6)} %convert_element_type.7, f32[1024,1024]{1,0:T(8,128)} %bitcast.9), kind=kOutput, calls=%fused_computation.15 | convolution fusion | flops 12885950464 | bytes 8388612 | tf_op jit(solution)/shard_map/dot_general | solution.py:38
  158.2 5.5 copy.42
  163.7 4.5 add_multiply_fusion
  168.3 2.0 copy-done.4
  170.3 11.7 %cholesky.236 = f32[128,128]{1,0:T(8,128)S(1)} custom-call(f32[128,128]{1,0:T(8,128)S(1)} %cholesky.612), custom_call_target="Cholesky" | custom-call | tf_op jit(solution)/shard_map/jit(cholesky)/cholesky | solution.py:41
  182.0 2.5 cholesky.266
  184.6 9.8 %custom-call.76 = f32[1,128,128]{1,2,0:T(8,128)S(1)} custom-call(f32[1,128,128]{2,1,0:T(8,128)S(1)} %get-tuple-element.44), custom_call_target="InvertDiagBlocksLowerTriangular" | custom-call | tf_op jit(solution)/shard_map/jit(cholesky)/cholesky | solution.py:41
  194.4 2.3 constant_dynamic-update-slice_fusion.50
  196.7 1.5 convolution_subtract_fusion
  198.2 11.9 %cholesky.259 = f32[128,128]{1,0:T(8,128)S(1)} custom-call(f32[128,128]{1,0:T(8,128)S(1)} %cholesky.616), custom_call_target="Cholesky" | custom-call | tf_op jit(solution)/shard_map/jit(cholesky)/cholesky | solution.py:41
  212.1 9.8 %custom-call.77 = f32[1,128,128]{1,2,0:T(8,128)S(1)} custom-call(f32[1,128,128]{2,1,0:T(8,128)S(1)} %get-tuple-element.41), custom_call_target="InvertDiagBlocksLowerTriangular" | custom-call | tf_op jit(solution)/shard_map/jit(cholesky)/cholesky | solution.py:41
  223.1 2.1 convolution_subtract_fusion.1
  225.2 11.7 %cholesky.492 = f32[128,128]{1,0:T(8,128)S(1)} custom-call(f32[128,128]{1,0:T(8,128)S(1)} %cholesky.621), custom_call_target="Cholesky" | custom-call | tf_op jit(solution)/shard_map/jit(cholesky)/cholesky | solution.py:41
  238.2 9.8 %custom-call.78 = f32[1,128,128]{1,2,0:T(8,128)S(1)} custom-call(f32[1,128,128]{2,1,0:T(8,128)S(1)} %get-tuple-element.38), custom_call_target="InvertDiagBlocksLowerTriangular" | custom-call | tf_op jit(solution)/shard_map/jit(cholesky)/cholesky | solution.py:41
  249.2 2.3 convolution_subtract_fusion.2
  251.5 12.1 %cholesky.511 = f32[128,128]{1,0:T(8,128)S(1)} custom-call(f32[128,128]{1,0:T(8,128)S(1)} %cholesky.626), custom_call_target="Cholesky" | custom-call | tf_op jit(solution)/shard_map/jit(cholesky)/cholesky | solution.py:41
  264.9 9.8 %custom-call.79 = f32[1,128,128]{1,2,0:T(8,128)S(1)} custom-call(f32[1,128,128]{2,1,0:T(8,128)S(1)} %get-tuple-element.35), custom_call_target="InvertDiagBlocksLowerTriangular" | custom-call | tf_op jit(solution)/shard_map/jit(cholesky)/cholesky | solution.py:41
  275.7 2.3 convolution_subtract_fusion.3
  278.1 11.7 %cholesky.530 = f32[128,128]{1,0:T(8,128)S(1)} custom-call(f32[128,128]{1,0:T(8,128)S(1)} %cholesky.631), custom_call_target="Cholesky" | custom-call | tf_op jit(solution)/shard_map/jit(cholesky)/cholesky | solution.py:41
  291.1 10.0 %custom-call.80 = f32[1,128,128]{1,2,0:T(8,128)S(1)} custom-call(f32[1,128,128]{2,1,0:T(8,128)S(1)} %get-tuple-element.32), custom_call_target="InvertDiagBlocksLowerTriangular" | custom-call | tf_op jit(solution)/shard_map/jit(cholesky)/cholesky | solution.py:41
  302.1 2.3 convolution_subtract_fusion.4
  304.4 11.7 %cholesky.550 = f32[128,128]{1,0:T(8,128)S(1)} custom-call(f32[128,128]{1,0:T(8,128)S(1)} %cholesky.636), custom_call_target="Cholesky" | custom-call | tf_op jit(solution)/shard_map/jit(cholesky)/cholesky | solution.py:41
  317.4 9.8 %custom-call.81 = f32[1,128,128]{1,2,0:T(8,128)S(1)} custom-call(f32[1,128,128]{2,1,0:T(8,128)S(1)} %get-tuple-element.29), custom_call_target="InvertDiagBlocksLowerTriangular" | custom-call | tf_op jit(solution)/shard_map/jit(cholesky)/cholesky | solution.py:41
  328.2 2.2 convolution_subtract_fusion.5
  330.4 11.9 %cholesky.570 = f32[128,128]{1,0:T(8,128)S(1)} custom-call(f32[128,128]{1,0:T(8,128)S(1)} %cholesky.641), custom_call_target="Cholesky" | custom-call | tf_op jit(solution)/shard_map/jit(cholesky)/cholesky | solution.py:41
  343.6 9.8 %custom-call.82 = f32[1,128,128]{1,2,0:T(8,128)S(1)} custom-call(f32[1,128,128]{2,1,0:T(8,128)S(1)} %get-tuple-element.26), custom_call_target="InvertDiagBlocksLowerTriangular" | custom-call | tf_op jit(solution)/shard_map/jit(cholesky)/cholesky | solution.py:41
  354.2 1.8 convolution_subtract_fusion.6
  356.0 11.7 %cholesky.588 = f32[128,128]{1,0:T(8,128)S(1)} custom-call(f32[128,128]{1,0:T(8,128)S(1)} %convolution_subtract_fusion.6), custom_call_target="Cholesky" | custom-call | tf_op jit(solution)/shard_map/jit(cholesky)/cholesky | solution.py:41
  374.0 4.9 select_select_fusion
  378.9 22.8 %while.1 = (s32[]{:T(128)}, f32[1024,1024]{1,0:T(8,128)}, s32[8,2]{0,1:T(2,128)S(1)}, f32[8,128,128]{2,1,0:T(8,128)S(1)}, s32[]{:T(128)}) while((s32[]{:T(128)}, f32[1024,1024]{1,0:T(8,128)}, s32[8,2]{0,1:T(2,128)S(1)}, f32[8,128,128]{2,1,0:T(8,128)S(1)}, s32[]{:T(128)}) %tuple.58), condition=%wide.while_cond, body=%wide.while_body.sunk | while | flops 2 | bytes 131181 | solution.py:42
  379.5 2.2 bitcast_dynamic-update-slice_fusion.2
  382.4 2.2 bitcast_dynamic-update-slice_fusion.2
  385.2 2.2 bitcast_dynamic-update-slice_fusion.2
  388.1 2.2 bitcast_dynamic-update-slice_fusion.2
  391.0 2.2 bitcast_dynamic-update-slice_fusion.2
  393.8 2.2 bitcast_dynamic-update-slice_fusion.2
  396.7 2.2 bitcast_dynamic-update-slice_fusion.2
  399.6 2.2 bitcast_dynamic-update-slice_fusion.2
  401.7 79.0 %custom-call.83 = f32[8,128,128]{1,2,0:T(8,128)S(1)} custom-call(f32[8,128,128]{2,1,0:T(8,128)S(1)} %get-tuple-element.12), custom_call_target="InvertDiagBlocksLowerTriangular" | custom-call | tf_op jit(solution)/shard_map/jit(_cho_solve)/triangular_solve | solution.py:42
  486.4 1.4 convolution_subtract_fusion.20
  488.0 1.5 convolution_subtract_fusion.19
  489.7 1.6 convolution_subtract_fusion.18
  500.3 1.4 convolution_subtract_fusion.15
  502.3 4.7 fusion.109
  507.0 5.3 copy.44
  512.4 2.7 cholesky.600
  516.6 2.3 custom-call.84
  519.5 6.6 bitcast_subtract_fusion
  526.1 5.5 copy.45
  531.6 5.0 gather_fusion.2
  536.6 2.6 fusion
  539.2 2.4 copy.46
  541.7 100.9 %all_to_all.38 = f32[1024,8,1,128]{3,1,2,0:T(8,128)S(1)} all-to-all(f32[1024,8,1,128]{3,1,2,0:T(8,128)S(1)} %copy.46), channel_id=1, replica_groups=mesh['chan'=32,'sky'=8] {'chan'}, dimensions={0} | all-to-all | bytes 8388608 | tf_op jit(solution)/shard_map/all_to_all | solution.py:73
  643.4 54.6 %all_to_all.39 = f32[32,8,32,128]{3,0,2,1:T(8,128)S(1)} all-to-all(f32[32,8,32,128]{3,0,2,1:T(8,128)S(1)} %copy.47), channel_id=1, replica_groups=mesh['chan'=32,'sky'=8] {'sky'}, dimensions={1} | all-to-all | bytes 8388608 | tf_op jit(solution)/shard_map/all_to_all | solution.py:72
  698.0 4.4 copy.48
  (149 shorter events, 46.4 us)
Async XLA Ops:
  0.0 6.7 copy-start
  0.0 8.3 %copy-start.2 = (s32[1,128]{1,0:T(1,128)S(1)}, s32[1,128]{1,0:T(1,128)}, u32[]{:S(2)}) copy-start(s32[1,128]{1,0:T(1,128)} %param.9) | copy-start | bytes 1540
  8.3 2.0 copy-start.3
  19.9 4.9 copy-start.7
  32.4 107.8 %all-to-all-start = ((f32[32,32,1024]{2,0,1:T(8,128)}), f32[32,32,1024]{2,0,1:T(8,128)}, u32[]{:S(2)}, u32[]{:S(2)}) async-start(f32[32,32,1024]{2,0,1:T(8,128)} %copy.41), calls=%async_computation | async-start | bytes 8388608 | tf_op jit(solution)/shard_map/all_to_all | solution.py:62
  158.2 5.5 copy-start.6
  168.3 2.0 copy-start.4
  374.0 106.8 %copy-start.5 = (f32[1024,30]{0,1:T(8,128)S(1)}, f32[1024,30]{0,1:T(8,128)}, u32[]{:S(2)}) copy-start(f32[1024,30]{0,1:T(8,128)} %param.7) | copy-start | bytes 368644
  643.4 59.0 %copy-start.1 = (f32[32,16384]{1,0:T(8,128)S(1)}, f32[32,16384]{1,0:T(8,128)}, u32[]{:S(2)}) copy-start(f32[32,16384]{1,0:T(8,128)} %param.6) | copy-start | bytes 6291460
where the time goes:
time: 711 us; the launch traced here: 703 us
  other arithmetic  276 us (39%)
  blocking collectives  155 us (22%)
  waiting for transfers between devices  94.8 us (13%)
  local copies, waits for them, and re-layouts  83.4 us (12%)
  matrix products  73.9 us (10%)
  starting transfers between devices  12.2 us (2%)
    another operation x31, other arithmetic, template_amplitudes(): factor = jnp.linalg.cholesky(covariance)  173 us
    all_to_all x1, blocking collectives, on_device(): lax.all_to_all(buffer, 'chan', split_axis=0, concat_axis=2, tiled=True)  101 us
    all_to_all x1, waiting for transfers between devices, on_device(): lax.all_to_all(outgoing, 'chan', split_axis=1, concat_axis=0, tiled=True)  94.8 us
    another operation x3, other arithmetic, template_amplitudes(): weighted = jax.scipy.linalg.cho_solve((factor, True), templates)  83.9 us
    all_to_all x1, blocking collectives, on_device(): lax.all_to_all(lax.all_to_all(buffer, 'chan', split_axis=0, concat_axis=2...  54.6 us
    another operation x25, local copies, waits for them, and re-layouts  23.4 us
    another operation x14, matrix products, template_amplitudes(): factor = jnp.linalg.cholesky(covariance)  23 us
    another operation x30, matrix products, template_amplitudes(): weighted = jax.scipy.linalg.cho_solve((factor, True), templates)  20.7 us
  transfers between devices with their start and end apart: 1, of which 1 were waited for; matrix products, arithmetic and copies ran while one was open for 0% of the time, Pallas kernels for 0%

commit v1 on v0

v1 whole, which is shorter than its diff:
```python
import functools
import jax, jax.numpy as jnp
from jax import lax
from jax.sharding import PartitionSpec as P
from jax.experimental import pallas as pl
from jax.experimental.pallas import tpu as pltpu
NU = 1024
BLK = 128
CAP = 8
HI = lax.Precision.HIGHEST
NT_DIMS = (((1,), (1,)), ((), ()))
NN_DIMS = (((1,), (0,)), ((), ()))

def mm_nn(a, b):
    return lax.dot_general(a, b, NN_DIMS, precision=HI, preferred_element_type=jnp.float32)

def invert_spd(ref, slabs):
    lane = lax.broadcasted_iota(jnp.int32, (8, 128), 1)
    sub = lax.broadcasted_iota(jnp.int32, (8, 128), 0)
    for t in range(slabs):
        lo = 8 * t
        in_slab = (lane >= lo) & (lane < lo + 8)
        rows = [jnp.broadcast_to(ref[lo + i:lo + i + 1, :], (8, 128)) for i in range(8)]
        a = {}
        for i in range(8):
            for j in range(i + 1):
                a[i, j] = jnp.broadcast_to(rows[i][:, lo + j:lo + j + 1], (8, 128))
        low, inv = {}, []
        for j in range(8):
            r = 1.0 / a[j, j]
            inv.append(r)
            for i in range(j + 1, 8):
                low[i, j] = a[i, j] * r
            for i in range(j + 1, 8):
                for m in range(j + 1, i + 1):
                    a[i, m] = a[i, m] - low[i, j] * a[m, j]
        y = []
        for i in range(8):
            v = jnp.where(in_slab, jnp.where(lane == lo + i, 1.0, 0.0), rows[i])
            for j in range(i):
                v = v - low[i, j] * y[j]
            y.append(v)
        u = [None] * 8
        for i in reversed(range(8)):
            v = y[i] * inv[i]
            for j in range(7, i, -1):
                v = v - low[j, i] * u[j]
            u[i] = v
        for g in list(range(t + 1, slabs)) + list(range(t)):
            row = ref[8 * g:8 * g + 8, :]
            acc = jnp.where(in_slab, 0.0, row)
            for j in range(8):
                acc = acc - jnp.broadcast_to(row[:, lo + j:lo + j + 1], (8, 128)) * u[j]
            ref[8 * g:8 * g + 8, :] = acc
        own = u[0]
        for i in range(1, 8):
            own = jnp.where(sub == i, u[i], own)
        ref[lo:lo + 8, :] = own

def split3(a):
    hi = a.astype(jnp.bfloat16)
    rest = a - hi.astype(jnp.float32)
    mid = rest.astype(jnp.bfloat16)
    low = (rest - mid.astype(jnp.float32)).astype(jnp.bfloat16)
    return hi, mid, low

def cat(parts):
    return jnp.concatenate(parts, axis=1)

def dot6(a, b, dims):
    def one(x, y):
        return lax.dot_general(x, y, dims, preferred_element_type=jnp.float32)
    if dims is NT_DIMS:
        return one(cat(a[:1]), b[2]) + one(cat(a[:2]), cat([b[1]] * 2)) + one(cat(a), cat([b[0]] * 3))
    up = lambda y, k: jnp.concatenate([y] * k, axis=0)
    return one(cat(a[:1]), b[2]) + one(cat(a[:2]), up(b[1], 2)) + one(cat(a), up(b[0], 3))

def gls_kernel(cnt_ref, x_ref, tt_ref, noise_ref, out_ref, xs_ref, q_ref, v_ref, p_ref, d_ref, w_ref, m_ref, nb=8):
    scale = 1.0 / (cnt_ref[0, 0] * 128).astype(jnp.float32)
    n = 128 * nb
    ext = n + 32
    row = lax.broadcasted_iota(jnp.int32, (128, 128), 0)
    col = lax.broadcasted_iota(jnp.int32, (128, 128), 1)

    def split_rows(r, carry):
        at = pl.ds(pl.multiple_of(r * 128, 128), 128)
        for i, part in enumerate(split3(x_ref[at, :])):
            xs_ref[i, at, :] = part
        return carry
    lax.fori_loop(0, nb, split_rows, 0)

    def factor(k):
        lo, hi = 128 * k, 128 * k + 128
        value = dot6(split3(p_ref[hi:ext, :]), split3(d_ref[...]), NN_DIMS)
        for i, part in enumerate(split3(value)):
            v_ref[i, hi:ext, lo:hi] = part

    def step(k, carry):
        for kk in range(nb):
            @pl.when(k == kk)
            def _(kk=kk):
                lo, hi = 128 * kk, 128 * kk + 128
                if kk:
                    factor(kk - 1)
                p_ref[n:ext, :] = tt_ref[:, lo:hi]
                p_ref[lo:n, :] = dot6([xs_ref[i, lo:n, :] for i in range(3)],
                                      [xs_ref[i, lo:hi, :] for i in range(3)], NT_DIMS) * scale
                if kk:
                    p_ref[lo:ext, :] -= dot6([v_ref[i, lo:ext, 0:lo] for i in range(3)],
                                             [q_ref[i, lo:hi, 0:lo] for i in range(3)], NT_DIMS)
                if hi < n:
                    for i, part in enumerate(split3(p_ref[hi:n, :])):
                        q_ref[i, hi:n, lo:hi] = part
                noise = jnp.broadcast_to(noise_ref[0:1, lo:hi], (128, 128))
                d_ref[...] = p_ref[lo:hi, :] + jnp.where(row == col, noise, 0.0)
        invert_spd(d_ref, 16)
        return carry
    lax.fori_loop(0, nb, step, 0)
    factor(nb - 1)
    for k in reversed(range(nb)):
        lo, hi = 128 * k, 128 * k + 128
        wk = sum(v_ref[i, n:ext, lo:hi].astype(jnp.float32) for i in (2, 1, 0))
        if hi < n:
            wk = wk - dot6([w_ref[i, :, hi:n] for i in range(3)],
                           [v_ref[i, hi:n, lo:hi] for i in range(3)], NN_DIMS)
        for i, part in enumerate(split3(wk)):
            w_ref[i, :, lo:hi] = part
    w = [w_ref[i] for i in range(3)]
    proj = dot6(w, [xs_ref[i] for i in range(3)], NN_DIMS)
    gram = dot6(w, split3(tt_pad(tt_ref, n)), NT_DIMS)
    prow = lax.broadcasted_iota(jnp.int32, (32, 128), 0)
    pcol = lax.broadcasted_iota(jnp.int32, (32, 128), 1)
    m_ref[...] = gram + jnp.where((prow == pcol) & (prow >= 30), 1.0, 0.0)
    invert_spd(m_ref, 4)
    out_ref[...] = mm_nn(m_ref[...][:, 0:32], proj)

def tt_pad(tt_ref, n):
    return jnp.concatenate([tt_ref[...], jnp.zeros((96, n), jnp.float32)], axis=0)

def gls(cnt, x, tt, noise):
    n = x.shape[0]
    nb = n // 128
    return pl.pallas_call(
        functools.partial(gls_kernel, nb=nb),
        out_shape=jax.ShapeDtypeStruct((32, x.shape[1]), jnp.float32),
        in_specs=[pl.BlockSpec(memory_space=pltpu.SMEM)] + [pl.BlockSpec(memory_space=pltpu.VMEM)] * 3,
        out_specs=pl.BlockSpec(memory_space=pltpu.VMEM),
        scratch_shapes=[pltpu.VMEM((3, n, n), jnp.bfloat16), pltpu.VMEM((3, n, n), jnp.bfloat16),
                        pltpu.VMEM((3, n + 32, n), jnp.bfloat16), pltpu.VMEM((n + 32, 128), jnp.float32),
                        pltpu.VMEM((128, 128), jnp.float32), pltpu.VMEM((3, 32, n), jnp.bfloat16),
                        pltpu.VMEM((32, 128), jnp.float32)],
        cost_estimate=pl.CostEstimate(flops=60 * 10**9, bytes_accessed=1 << 22, transcendentals=0),
        compiler_params=pltpu.CompilerParams(vmem_limit_bytes=40 << 20),
    )(cnt, x, tt, noise)


def pack_kernel(slot_ref, slab_ref, map_ref, out_ref, sky_ref):
    def put(c, carry):
        for j in range(CAP):
            block = slot_ref[c, j]
            at = pl.multiple_of(jnp.maximum(block, 0) * BLK, BLK)
            tile = map_ref[:, pl.ds(at, BLK)]
            out_ref[c, :, j * BLK:(j + 1) * BLK] = jnp.where(block >= 0, tile, 0.0)
        place = pl.multiple_of(c * BLK, BLK)
        for d in range(sky_ref.shape[0]):
            block = slab_ref[d, c]
            at = pl.multiple_of(jnp.maximum(block, 0) * BLK, BLK)
            tile = map_ref[:, pl.ds(at, BLK)]
            sky_ref[d, :, pl.ds(place, BLK)] = jnp.where(block >= 0, tile, 0.0)
        return carry
    lax.fori_loop(0, slot_ref.shape[0], put, 0)


def pack(slot_block, slab_block, sky_map):
    owners, rows = slot_block.shape[0], sky_map.shape[0]
    slabs = slab_block.shape[0]
    return pl.pallas_call(
        pack_kernel,
        out_shape=(jax.ShapeDtypeStruct((owners, rows, CAP * BLK), jnp.float32),
                   jax.ShapeDtypeStruct((slabs, rows, owners * BLK), jnp.float32)),
        in_specs=[pl.BlockSpec(memory_space=pltpu.SMEM)] * 2 + [pl.BlockSpec(memory_space=pltpu.VMEM)],
        out_specs=(pl.BlockSpec(memory_space=pltpu.VMEM),) * 2,
        compiler_params=pltpu.CompilerParams(vmem_limit_bytes=40 << 20),
    )(slot_block, slab_block, sky_map)


RINGS = (8, 4)
SPLIT = 5


def gather_plan(cost):
    time, free, queue, serial = 0.0, {}, [], 0
    events = []

    def send(now, part, axis, off, sign, hop):
        nonlocal serial
        half = hop == RINGS[axis] // 2
        groups = SPLIT if part == 0 else 8 - SPLIT
        link = (axis, sign)
        start = max(now, free.get(link, 0.0))
        free[link] = start + cost * groups * (0.5 if half else 1.0)
        serial += 1
        queue.append((free[link] + 2.0, serial, (part, axis, off, sign, hop)))
        return part, axis, off, sign, hop

    def both(now, part, axis, off):
        return [send(now, part, axis, off, sign, 1) for sign in (1, -1)]

    first = []
    for part in (0, 1):
        first += both(0.0, part, part, (0, 0))
    for part in (0, 1):
        first += both(0.0, part, 1 - part, (0, 0))
    halves = set()
    while queue:
        queue.sort()
        time, _, (part, axis, off, sign, hop) = queue.pop(0)
        moved = list(off)
        moved[axis] -= sign
        moved = tuple(moved)
        half = hop == RINGS[axis] // 2
        out = []
        if not half:
            out.append(send(time, part, axis, moved, sign, hop + 1))
        if axis == part:
            place = (part, moved[axis] % RINGS[axis])
            if not half or place in halves:
                out += both(time, part, 1 - axis, moved)
            halves.add(place)
        events.append(((part, axis, off, sign, hop), moved, out))
    return first, events, time


def gather_kernel(amp_ref, out_ref, local_sem, send_sem, recv_sem):
    chan = lax.axis_index("chan")
    place = (chan // RINGS[1], lax.rem(chan, RINGS[1]))

    def member(off):
        at = [lax.rem(place[i] + off[i] % RINGS[i], RINGS[i]) for i in (0, 1)]
        return at[0] * RINGS[1] + at[1]

    first, events, _ = gather_plan(1.0)
    number = {event[0]: k for k, event in enumerate(events)}

    def copy(key, off):
        part, axis, start, sign, hop = key
        half = hop == RINGS[axis] // 2
        groups = slice(0, SPLIT) if part == 0 else slice(SPLIT, 8)
        rows = slice(0, 32)
        if half:
            rows = slice(0, 16) if sign > 0 else slice(16, 32)
        k = number[key]
        chunk = member(off)
        step = [0, 0]
        step[axis] = sign
        own = off == (0, 0)
        src = amp_ref.at[groups, rows] if own else out_ref.at[chunk, groups, rows]
        return pltpu.make_async_remote_copy(
            src_ref=src, dst_ref=out_ref.at[chunk, groups, rows], send_sem=send_sem.at[k], recv_sem=recv_sem.at[k],
            device_id={"chan": member(step)}, device_id_type=pl.DeviceIdType.MESH)

    barrier = pltpu.get_barrier_semaphore()
    for step in ((1, 0), (-1, 0), (0, 1), (0, -1)):
        pl.semaphore_signal(barrier, inc=1, device_id={"chan": member(step)},
                            device_id_type=pl.DeviceIdType.MESH)
    pl.semaphore_wait(barrier, 4)
    sent = [copy(key, key[2]) for key in first]
    for c in sent:
        c.start()
    local = pltpu.make_async_copy(amp_ref, out_ref.at[chan], local_sem)
    local.start()
    for key, moved, out in events:
        copy(key, moved).wait_recv()
        for nxt in out:
            c = copy(nxt, nxt[2])
            c.start()
            sent.append(c)
    local.wait()
    for c in sent:
        c.wait_send()


def gather(amp):
    count = len(gather_plan(1.0)[1])
    return pl.pallas_call(
        gather_kernel,
        out_shape=jax.ShapeDtypeStruct((RINGS[0] * RINGS[1],) + amp.shape, jnp.float32),
        in_specs=[pl.BlockSpec(memory_space=pltpu.VMEM)],
        out_specs=pl.BlockSpec(memory_space=pltpu.VMEM),
        scratch_shapes=[pltpu.SemaphoreType.DMA, pltpu.SemaphoreType.DMA((count,)), pltpu.SemaphoreType.DMA((count,))],
        compiler_params=pltpu.CompilerParams(collective_id=0, has_side_effects=True, vmem_limit_bytes=40 << 20),
    )(amp)


def clean_kernel(tmpl_ref, amp_ref, raw_ref, out_ref):
    owners = amp_ref.shape[0]
    for c in range(0, owners, 8):
        amp = jnp.concatenate([amp_ref[c + i, 0] for i in range(8)], axis=1)
        rest = raw_ref[0, :, c * BLK:(c + 8) * BLK] - mm_nn(tmpl_ref[...], amp)
        for i in range(8):
            out_ref[:, c + i, :] = rest[:, i * BLK:(i + 1) * BLK]


def clean(tmpl, amp, raw):
    owners, groups = amp.shape[0], amp.shape[1]
    rows = raw.shape[1]
    return pl.pallas_call(
        clean_kernel,
        grid=(groups,),
        out_shape=jax.ShapeDtypeStruct((rows, groups * owners, BLK), jnp.float32),
        in_specs=[pl.BlockSpec(tmpl.shape, lambda g: (0, 0)),
                  pl.BlockSpec((owners, 1, amp.shape[2], BLK), lambda g: (0, g, 0, 0)),
                  pl.BlockSpec((1, rows, owners * BLK), lambda g: (g, 0, 0))],
        out_specs=pl.BlockSpec((rows, owners, BLK), lambda g: (0, g, 0)),
    )(tmpl, amp, raw)


def tables(order_row, counts_row, dest_rows, slabs):
    slot_index = jnp.arange(CAP, dtype=jnp.int32)
    offsets = jnp.cumsum(counts_row) - counts_row
    live = slot_index[None, :] < counts_row[:, None]
    position = jnp.where(live, offsets[:, None] + slot_index[None, :], 0)
    slot_block = jnp.where(live, jnp.take(order_row, position, axis=0), -1)
    bound = dest_rows[None, :, :] == jnp.arange(slabs, dtype=jnp.int32)[:, None, None]
    slab_block = jnp.max(jnp.where(bound, slot_block[None, :, :], -1), axis=2)
    return slot_block.astype(jnp.int32), slab_block.astype(jnp.int32)


def on_device(sky_map, templates, noise_var, block_order, patch_count, slab_dest):
    slabs = lax.axis_size("sky")
    member = lax.axis_index("chan")
    rows = sky_map.shape[0]
    slot_block, slab_block = tables(block_order[0], patch_count[0], slab_dest[0], slabs)
    outgoing, sky_out = pack(slot_block, slab_block, sky_map)
    pixels = lax.all_to_all(outgoing, "chan", split_axis=0, concat_axis=0, tiled=True)
    pixels = pixels.reshape(NU, CAP * BLK)
    pixels, sky_out = lax.optimization_barrier((pixels, sky_out))
    raw = lax.all_to_all(sky_out, "sky", split_axis=0, concat_axis=0, tiled=True)
    block_count = lax.dynamic_index_in_dim(patch_count[0], member, 0, keepdims=False)
    padded = jnp.pad(templates, ((0, 0), (0, 32 - templates.shape[1])))
    amp = gls(block_count.reshape(1, 1), pixels, padded.T, noise_var[None, :])
    amp, raw = lax.optimization_barrier((amp, raw))
    own_dest = lax.dynamic_index_in_dim(slab_dest[0], member, 0, keepdims=False)
    slot_index = jnp.arange(CAP, dtype=jnp.int32)
    match = (own_dest[None, :] == jnp.arange(slabs, dtype=jnp.int32)[:, None]) & (slot_index[None, :] < block_count)
    source = jnp.sum(jnp.where(match, slot_index[None, :], 0), axis=1)
    amp = jnp.take(amp.reshape(32, CAP, BLK).transpose(1, 0, 2), source, axis=0)
    amp = jnp.where(jnp.any(match, axis=1)[:, None, None], amp, 0.0)
    amp = lax.all_to_all(amp, "sky", split_axis=0, concat_axis=0, tiled=True)
    amp = gather(amp)
    own = lax.dynamic_slice_in_dim(padded, member * rows, rows, 0)
    return clean(own, amp, raw)


def solution(mesh):
    return jax.shard_map(
        on_device,
        mesh=mesh,
        in_specs=(P("chan", "sky"), P(), P(), P("sky", None), P("sky", None), P("sky", None, None)),
        out_specs=P("chan", "sky", None),
        check_vma=False,
    )
```

time: 711 us -> 249 us (0.35); the launches traced: 703 us -> 248 us
  other arithmetic: 276 us -> 3.29 us
  blocking collectives: 155 us -> 0 us
  Pallas kernels: 0 us -> 113 us
  matrix products: 73.9 us -> 0 us
  local copies, waits for them, and re-layouts: 83.4 us -> 11.2 us
  starting transfers between devices: 12.2 us -> 21 us
    another operation x41 -> x2, other arithmetic: 264 us -> 0.17 us  [the longest x31 173 us: template_amplitudes(): factor = jnp.linalg.cholesky(covariance)]
    all_to_all x2 -> x0, blocking collectives: 155 us -> none  [the longest x1 101 us: on_device(): lax.all_to_all(buffer, 'chan', split_axis=0, concat_axis=2, tiled=True)]
    pallas_call x0 -> x4, Pallas kernels: none -> 113 us  [the longest x1 67.8 us: gls(): pl.pallas_call(functools.partial(gls_kernel, nb=nb), out_shape=jax.ShapeD...]
    another operation x46 -> x0, matrix products: 44.4 us -> none  [the longest x14 23 us: template_amplitudes(): factor = jnp.linalg.cholesky(covariance)]
    dot_general x4 -> x0, matrix products: 29.6 us -> none  [the longest x1 18.1 us: template_amplitudes(): jnp.dot(pixels, pixels.T, precision=highest)]
    another operation x38 -> x1, local copies, waits for them, and re-layouts: 26 us -> 0.75 us
    gather x6 -> x3, local copies, waits for them, and re-layouts: 21.5 us -> 2.5 us  [the longest x2 1.95 us: tables(): slot_block = jnp.where(live, jnp.take(order_row, position, axis=0), -1)]
    reshape x3 -> x0, local copies, waits for them, and re-layouts: 12.4 us -> none  [the longest x1 5.47 us: on_device(): buffer = jnp.take(cleaned.reshape(NU, CAP, BLK), source_slot, axis=1)]
  transfers between devices with their start and end apart: 1 -> 3, of which waited for: 1 -> 2; matrix products, arithmetic and copies ran while one was open for 0% -> 1% of each run, Pallas kernels for 0% -> 27%
where the time goes in v1:
time: 249 us; the launch traced here: 248 us
  Pallas kernels  113 us (45%)
  waiting for transfers between devices  99.2 us (40%)
  starting transfers between devices  21 us (8%)
  local copies, waits for them, and re-layouts  11.2 us (4%)
  other arithmetic  3.29 us (1%)
    all_to_all x1, waiting for transfers between devices, on_device(): lax.all_to_all(outgoing, 'chan', split_axis=0, concat_axis=0, tiled=True)  93.6 us
    pallas_call x1, Pallas kernels, gls(): pl.pallas_call(functools.partial(gls_kernel, nb=nb), out_shape=jax.ShapeD...  67.8 us
    pallas_call x1, Pallas kernels, gather(): pl.pallas_call(gather_kernel, out_shape=jax.ShapeDtypeStruct((RINGS[0] *...  32.9 us
    all_to_all x1, starting transfers between devices, on_device(): lax.all_to_all(outgoing, 'chan', split_axis=0, concat_axis=0, tiled=True)  11.7 us
    pallas_call x1, Pallas kernels, clean(): pl.pallas_call(clean_kernel, grid=(groups,), out_shape=jax.ShapeDtypeStru...  9.8 us
    unnamed x19, local copies, waits for them, and re-layouts  6.18 us
    all_to_all x1, waiting for transfers between devices, on_device(): amp = lax.all_to_all(amp, 'sky', split_axis=0, concat_axis=0, tiled=True)  5.53 us
  transfers between devices with their start and end apart: 3, of which 2 were waited for; matrix products, arithmetic and copies ran while one was open for 1% of the time, Pallas kernels for 27%

profile of v1, /device:TPU:24, one launch (start us, length us, event | category | flops | bytes accessed | tf_op | source)
XLA Modules:
  0.0 248.1 jit_solution(17455216270764687224)
XLA Ops:
  0.0 0.0 copy-start
  0.0 0.7 copy.17
  0.8 0.1 reduce-window.8
  0.8 0.1 reduce.1
  0.9 0.7 bitcast_subtract_fusion
  1.6 0.7 compare_select_fusion
  2.3 0.1 reshape.232
  2.4 0.0 copy-done
  2.4 0.0 copy-start.8
  2.4 0.0 copy-start.7
  2.5 0.0 copy-start.4
  2.5 1.9 gather_fusion
  4.3 0.1 reshape.231
  4.4 0.0 copy-done.8
  4.4 0.1 select_select_fusion.1.slot_ref
  4.5 0.1 copy.18
  4.6 0.0 copy-done.7
  4.6 0.0 copy-done.4
  4.6 2.8 %shard_map.64 = (f32[32,32,1024]{2,1,0:T(8,128)S(1)}, f32[8,32,4096]{2,1,0:T(8,128)S(1)}) custom-call(s32[32,8]{1,0:T(8,128)S(1)} %select_select_fusion.1.slot_ref, s32[8,32]{1,0:T(8,128)S(1)} %select_reduce_fusion.slab_ref, f32[32,16384]{1,0:T(8,128)S(1)} %copy-done.4), custom_call_target="tpu_custom_call" | custom-call | tf_op jit(solution)/shard_map/pallas_call | solution.py:177
  7.4 0.0 copy-start.2
  7.4 2.0 copy-done.2
  9.4 0.0 copy-start.3
  9.4 2.0 copy-done.3
  11.4 0.0 copy-start.6
  11.4 11.7 %all-to-all-start = ((f32[32,32,1024]{2,1,0:T(8,128)}), f32[32,32,1024]{2,1,0:T(8,128)}, u32[]{:S(2)}, u32[]{:S(2)}) async-start(f32[32,32,1024]{2,1,0:T(8,128)} %copy-done.3), calls=%async_computation | async-start | bytes 8388608 | tf_op jit(solution)/shard_map/all_to_all | solution.py:335
  23.0 0.6 constant_dynamic-slice_fusion.cnt_ref
  23.7 0.2 dynamic-slice_reduce_fusion
  23.8 0.0 copy-done.6
  23.8 0.2 copy.16
  24.1 0.2 copy.19.tt_ref
  24.3 0.6 iota_compare_fusion.4
  24.9 0.1 select_reduce_fusion.1
  25.0 0.1 fusion.4
  25.2 93.6 %all-to-all-done = f32[32,32,1024]{2,1,0:T(8,128)} async-done(((f32[32,32,1024]{2,1,0:T(8,128)}), f32[32,32,1024]{2,1,0:T(8,128)}, u32[]{:S(2)}, u32[]{:S(2)}) %all-to-all-start) | async-done | bytes 4194336 | tf_op jit(solution)/shard_map/all_to_all | solution.py:335
  118.8 0.0 copy-start.5
  118.8 4.7 %all-to-all-start.1 = ((f32[8,32,4096]{2,1,0:T(8,128)}), f32[8,32,4096]{2,1,0:T(8,128)}, u32[]{:S(2)}, u32[]{:S(2)}) async-start(f32[8,32,4096]{2,1,0:T(8,128)} %copy-done.2), calls=%async_computation.1 | async-start | bytes 8388608 | tf_op jit(solution)/shard_map/all_to_all | solution.py:338
  123.5 0.0 copy-done.5
  123.5 67.8 %shard_map.65 = f32[32,1024]{1,0:T(8,128)S(1)} custom-call(s32[1,1]{1,0:T(1,128)} %constant_dynamic-slice_fusion.cnt_ref, f32[1024,1024]{1,0:T(8,128)} %bitcast.5.x_ref, f32[32,1024]{1,0:T(8,128)S(1)} %copy.19.tt_ref, f32[1,1024]{1,0:T(1,128)S(1)} %bitcast.24), custom_call_target="tpu_custom_call" | custom-call | flops 60000002048 | bytes 4194304 | tf_op jit(solution)/shard_map/pallas_call | solution.py:143
  191.3 0.0 all-to-all-done.1.raw_ref
  191.4 0.6 gather_fusion.1
  191.9 0.7 select_select_fusion
  192.7 4.7 %all-to-all-start.2 = ((f32[8,32,128]{2,1,0:T(8,128)}), f32[8,32,128]{2,1,0:T(8,128)S(1)}, u32[]{:S(2)}, u32[]{:S(2)}) async-start(f32[8,32,128]{2,1,0:T(8,128)} %select_select_fusion), calls=%async_computation.2 | async-start | bytes 262144 | tf_op jit(solution)/shard_map/all_to_all | solution.py:349
  197.4 0.6 pad_dynamic-slice_fusion.tmpl_ref
  198.0 5.5 %all-to-all-done.2.amp_ref = f32[8,32,128]{2,1,0:T(8,128)S(1)} async-done(((f32[8,32,128]{2,1,0:T(8,128)}), f32[8,32,128]{2,1,0:T(8,128)S(1)}, u32[]{:S(2)}, u32[]{:S(2)}) %all-to-all-start.2) | async-done | bytes 131104 | tf_op jit(solution)/shard_map/all_to_all | solution.py:349
  203.5 32.9 %shard_map.66.amp_ref = f32[32,8,32,128]{3,2,1,0:T(8,128)S(1)} custom-call(f32[8,32,128]{2,1,0:T(8,128)S(1)} %all-to-all-done.2.amp_ref), custom_call_target="tpu_custom_call" | custom-call | tf_op jit(solution)/shard_map/pallas_call | solution.py:285
  236.4 0.0 copy-start.1
  236.4 2.0 copy-done.1
  238.3 9.8 %shard_map.67 = f32[32,256,128]{2,1,0:T(8,128)} custom-call(f32[32,32]{1,0:T(8,128)} %pad_dynamic-slice_fusion.tmpl_ref, f32[32,8,32,128]{3,2,1,0:T(8,128)} %copy-done.1, f32[8,32,4096]{2,1,0:T(8,128)} %all-to-all-done.1.raw_ref), custom_call_target="tpu_custom_call" | custom-call | tf_op jit(solution)/shard_map/pallas_call | solution.py:307
  (7 shorter events, 0.1 us)
Async XLA Ops:
  0.0 2.4 copy-start
  2.4 2.0 copy-start.8
  2.4 2.1 copy-start.7
  2.5 2.2 copy-start.4
  7.4 2.0 copy-start.2
  9.4 2.0 copy-start.3
  11.4 12.5 %copy-start.6 = (f32[1024,30]{0,1:T(8,128)S(1)}, f32[1024,30]{0,1:T(8,128)}, u32[]{:S(2)}) copy-start(f32[1024,30]{0,1:T(8,128)} %param.7) | copy-start | bytes 368644
  11.4 107.4 %all-to-all-start = ((f32[32,32,1024]{2,1,0:T(8,128)}), f32[32,32,1024]{2,1,0:T(8,128)}, u32[]{:S(2)}, u32[]{:S(2)}) async-start(f32[32,32,1024]{2,1,0:T(8,128)} %copy-done.3), calls=%async_computation | async-start | bytes 8388608 | tf_op jit(solution)/shard_map/all_to_all | solution.py:335
  118.8 4.7 %copy-start.5 = (f32[1024]{0:T(1024)S(1)}, f32[1024]{0:T(1024)}, u32[]{:S(2)}) copy-start(f32[1024]{0:T(1024)} %param.8) | copy-start | bytes 12292
  118.8 72.6 %all-to-all-start.1 = ((f32[8,32,4096]{2,1,0:T(8,128)}), f32[8,32,4096]{2,1,0:T(8,128)}, u32[]{:S(2)}, u32[]{:S(2)}) async-start(f32[8,32,4096]{2,1,0:T(8,128)} %copy-done.2), calls=%async_computation.1 | async-start | bytes 8388608 | tf_op jit(solution)/shard_map/all_to_all | solution.py:338
  192.7 10.8 %all-to-all-start.2 = ((f32[8,32,128]{2,1,0:T(8,128)}), f32[8,32,128]{2,1,0:T(8,128)S(1)}, u32[]{:S(2)}, u32[]{:S(2)}) async-start(f32[8,32,128]{2,1,0:T(8,128)} %select_select_fusion), calls=%async_computation.2 | async-start | bytes 262144 | tf_op jit(solution)/shard_map/all_to_all | solution.py:349
  236.4 2.0 copy-start.1

commit v2 on v1

--- a/solution.py
+++ b/solution.py
@@ -154,34 +154,38 @@
     )(cnt, x, tt, noise)
 
 
-def pack_kernel(slot_ref, slab_ref, map_ref, out_ref, sky_ref):
+def slot_kernel(slot_ref, map_ref, out_ref):
     def put(c, carry):
         for j in range(CAP):
             block = slot_ref[c, j]
             at = pl.multiple_of(jnp.maximum(block, 0) * BLK, BLK)
             tile = map_ref[:, pl.ds(at, BLK)]
             out_ref[c, :, j * BLK:(j + 1) * BLK] = jnp.where(block >= 0, tile, 0.0)
+        return carry
+    lax.fori_loop(0, slot_ref.shape[0], put, 0)
+
+
+def slab_kernel(slab_ref, map_ref, out_ref):
+    def put(c, carry):
         place = pl.multiple_of(c * BLK, BLK)
-        for d in range(sky_ref.shape[0]):
+        for d in range(out_ref.shape[0]):
             block = slab_ref[d, c]
             at = pl.multiple_of(jnp.maximum(block, 0) * BLK, BLK)
             tile = map_ref[:, pl.ds(at, BLK)]
-            sky_ref[d, :, pl.ds(place, BLK)] = jnp.where(block >= 0, tile, 0.0)
+            out_ref[d, :, pl.ds(place, BLK)] = jnp.where(block >= 0, tile, 0.0)
         return carry
-    lax.fori_loop(0, slot_ref.shape[0], put, 0)
-
-
-def pack(slot_block, slab_block, sky_map):
-    owners, rows = slot_block.shape[0], sky_map.shape[0]
-    slabs = slab_block.shape[0]
+    lax.fori_loop(0, slab_ref.shape[1], put, 0)
+
+
+def pack(kernel, blocks, shape, sky_map):
     return pl.pallas_call(
-        pack_kernel,
-        out_shape=(jax.ShapeDtypeStruct((owners, rows, CAP * BLK), jnp.float32),
-                   jax.ShapeDtypeStruct((slabs, rows, owners * BLK), jnp.float32)),
-        in_specs=[pl.BlockSpec(memory_space=pltpu.SMEM)] * 2 + [pl.BlockSpec(memory_space=pltpu.VMEM)],
-        out_specs=(pl.BlockSpec(memory_space=pltpu.VMEM),) * 2,
+        kernel,
+        out_shape=jax.ShapeDtypeStruct(shape, jnp.float32),
+        in_specs=[pl.BlockSpec(memory_space=pltpu.SMEM), pl.BlockSpec(memory_space=pltpu.VMEM)],
+        out_specs=pl.BlockSpec(memory_space=pltpu.VMEM),
+        cost_estimate=pl.CostEstimate(flops=10**6, bytes_accessed=6 << 20, transcendentals=0),
         compiler_params=pltpu.CompilerParams(vmem_limit_bytes=40 << 20),
-    )(slot_block, slab_block, sky_map)
+    )(blocks, sky_map)
 
 
 RINGS = (8, 4)
@@ -231,8 +235,10 @@
     return first, events, time
 
 
-def gather_kernel(amp_ref, out_ref, local_sem, send_sem, recv_sem):
+def gather_kernel(amp_ref, out_ref, own_ref, local_sem, send_sem, recv_sem, sky_send_sem, sky_recv_sem):
     chan = lax.axis_index("chan")
+    sky = lax.axis_index("sky")
+    slabs = amp_ref.shape[0]
     place = (chan // RINGS[1], lax.rem(chan, RINGS[1]))
 
     def member(off):
@@ -254,7 +260,7 @@
         step = [0, 0]
         step[axis] = sign
         own = off == (0, 0)
-        src = amp_ref.at[groups, rows] if own else out_ref.at[chunk, groups, rows]
+        src = own_ref.at[groups, rows] if own else out_ref.at[chunk, groups, rows]
         return pltpu.make_async_remote_copy(
             src_ref=src, dst_ref=out_ref.at[chunk, groups, rows], send_sem=send_sem.at[k], recv_sem=recv_sem.at[k],
             device_id={"chan": member(step)}, device_id_type=pl.DeviceIdType.MESH)
@@ -263,11 +269,30 @@
     for step in ((1, 0), (-1, 0), (0, 1), (0, -1)):
         pl.semaphore_signal(barrier, inc=1, device_id={"chan": member(step)},
                             device_id_type=pl.DeviceIdType.MESH)
-    pl.semaphore_wait(barrier, 4)
+    for k in range(1, slabs):
+        pl.semaphore_signal(barrier, inc=1, device_id={"sky": lax.rem(sky + k, slabs)},
+                            device_id_type=pl.DeviceIdType.MESH)
+    pl.semaphore_wait(barrier, 3 + slabs)
+
+    def exchange(k):
+        to, source = lax.rem(sky + k, slabs), lax.rem(sky + slabs - k, slabs)
+        out, landed = [pltpu.make_async_remote_copy(
+            src_ref=amp_ref.at[to], dst_ref=own_ref.at[at], send_sem=sky_send_sem.at[k], recv_sem=sky_recv_sem.at[k],
+            device_id={"sky": to}, device_id_type=pl.DeviceIdType.MESH) for at in (sky, source)]
+        return out, landed
+
+    swaps = [exchange(k) for k in range(1, slabs)]
+    for out, _ in swaps:
+        out.start()
+    kept = pltpu.make_async_copy(amp_ref.at[sky], own_ref.at[sky], local_sem)
+    kept.start()
+    kept.wait()
+    for _, landed in swaps:
+        landed.wait_recv()
     sent = [copy(key, key[2]) for key in first]
     for c in sent:
         c.start()
-    local = pltpu.make_async_copy(amp_ref, out_ref.at[chan], local_sem)
+    local = pltpu.make_async_copy(own_ref, out_ref.at[chan], local_sem)
     local.start()
     for key, moved, out in events:
         copy(key, moved).wait_recv()
@@ -278,6 +303,8 @@
     local.wait()
     for c in sent:
         c.wait_send()
+    for out, _ in swaps:
+        out.wait_send()
 
 
 def gather(amp):
@@ -287,7 +314,9 @@
         out_shape=jax.ShapeDtypeStruct((RINGS[0] * RINGS[1],) + amp.shape, jnp.float32),
         in_specs=[pl.BlockSpec(memory_space=pltpu.VMEM)],
         out_specs=pl.BlockSpec(memory_space=pltpu.VMEM),
-        scratch_shapes=[pltpu.SemaphoreType.DMA, pltpu.SemaphoreType.DMA((count,)), pltpu.SemaphoreType.DMA((count,))],
+        scratch_shapes=[pltpu.VMEM(amp.shape, jnp.float32), pltpu.SemaphoreType.DMA, pltpu.SemaphoreType.DMA((count,)),
+                        pltpu.SemaphoreType.DMA((count,)), pltpu.SemaphoreType.DMA((8,)),
+                        pltpu.SemaphoreType.DMA((8,))],
         compiler_params=pltpu.CompilerParams(collective_id=0, has_side_effects=True, vmem_limit_bytes=40 << 20),
     )(amp)
 
@@ -331,7 +360,9 @@
     member = lax.axis_index("chan")
     rows = sky_map.shape[0]
     slot_block, slab_block = tables(block_order[0], patch_count[0], slab_dest[0], slabs)
-    outgoing, sky_out = pack(slot_block, slab_block, sky_map)
+    owners = slot_block.shape[0]
+    outgoing = pack(slot_kernel, slot_block, (owners, rows, CAP * BLK), sky_map)
+    sky_out = pack(slab_kernel, slab_block, (slabs, rows, owners * BLK), sky_map)
     pixels = lax.all_to_all(outgoing, "chan", split_axis=0, concat_axis=0, tiled=True)
     pixels = pixels.reshape(NU, CAP * BLK)
     pixels, sky_out = lax.optimization_barrier((pixels, sky_out))
@@ -346,7 +377,6 @@
     source = jnp.sum(jnp.where(match, slot_index[None, :], 0), axis=1)
     amp = jnp.take(amp.reshape(32, CAP, BLK).transpose(1, 0, 2), source, axis=0)
     amp = jnp.where(jnp.any(match, axis=1)[:, None, None], amp, 0.0)
-    amp = lax.all_to_all(amp, "sky", split_axis=0, concat_axis=0, tiled=True)
     amp = gather(amp)
     own = lax.dynamic_slice_in_dim(padded, member * rows, rows, 0)
     return clean(own, amp, raw)

time: 249 us -> 240 us (0.964)
  waiting for transfers between devices: 99.2 us -> 89.2 us
  Pallas kernels: 113 us -> 119 us
  starting transfers between devices: 21 us -> 16.3 us
    all_to_all x1 -> x0, waiting for transfers between devices: 5.53 us -> none  [on_device(): amp = lax.all_to_all(amp, 'sky', split_axis=0, concat_axis=0, tiled=True)]
    pallas_call x1, Pallas kernels: 32.9 us -> 38.2 us  [gather(): pl.pallas_call(gather_kernel, out_shape=jax.ShapeDtypeStruct((RINGS[0] *...]
    all_to_all x1 -> x0, starting transfers between devices: 4.69 us -> none  [on_device(): amp = lax.all_to_all(amp, 'sky', split_axis=0, concat_axis=0, tiled=True)]
    all_to_all x1, waiting for transfers between devices: 93.6 us -> 89.2 us  [on_device(): lax.all_to_all(outgoing, 'chan', split_axis=0, concat_axis=0, tiled=True)]
  transfers between devices with their start and end apart: 3 -> 2, of which waited for: 2 -> 1; matrix products, arithmetic and copies ran while one was open for 1% -> 1% of each run, Pallas kernels for 27% -> 29%
where the time goes in v2:
time: 240 us; the launch traced here: 239 us
  Pallas kernels  119 us (50%)
  waiting for transfers between devices  89.2 us (37%)
  starting transfers between devices  16.3 us (7%)
  local copies, waits for them, and re-layouts  11.2 us (5%)
  other arithmetic  2.7 us (1%)
    all_to_all x1, waiting for transfers between devices, on_device(): lax.all_to_all(outgoing, 'chan', split_axis=0, concat_axis=0, tiled=True)  89.2 us
    pallas_call x1, Pallas kernels, gls(): pl.pallas_call(functools.partial(gls_kernel, nb=nb), out_shape=jax.ShapeD...  67.9 us
    pallas_call x1, Pallas kernels, gather(): pl.pallas_call(gather_kernel, out_shape=jax.ShapeDtypeStruct((RINGS[0] *...  38.2 us
    all_to_all x1, starting transfers between devices, on_device(): lax.all_to_all(outgoing, 'chan', split_axis=0, concat_axis=0, tiled=True)  11.7 us
    pallas_call x1, Pallas kernels, clean(): pl.pallas_call(clean_kernel, grid=(groups,), out_shape=jax.ShapeDtypeStru...  9.8 us
    unnamed x19, local copies, waits for them, and re-layouts  6.18 us
  transfers between devices with their start and end apart: 2, of which 1 were waited for; matrix products, arithmetic and copies ran while one was open for 1% of the time, Pallas kernels for 29%

profile of v2, /device:TPU:24, one launch (start us, length us, event | category | flops | bytes accessed | tf_op | source)
XLA Modules:
  0.0 239.1 jit_solution(11782120996303193073)
XLA Ops:
  0.0 0.0 copy-start
  0.0 0.7 copy.17
  0.8 0.1 reduce-window.8
  0.8 0.1 reduce.1
  0.9 0.7 bitcast_subtract_fusion
  1.6 0.7 compare_select_fusion
  2.3 0.1 reshape.232
  2.4 0.0 copy-done
  2.4 0.0 copy-start.8
  2.4 0.0 copy-start.4
  2.5 1.9 gather_fusion
  4.3 0.1 reshape.231
  4.4 0.0 copy-done.8
  4.4 0.1 select_select_fusion.1.slot_ref
  4.5 0.0 copy-done.4
  4.5 1.8 shard_map.64
  6.4 0.0 copy-start.1
  6.4 2.0 copy-done.1
  8.4 0.0 copy-start.7
  8.4 0.0 copy-start.6
  8.4 11.7 %all-to-all-start = ((f32[32,32,1024]{2,1,0:T(8,128)}), f32[32,32,1024]{2,1,0:T(8,128)}, u32[]{:S(2)}, u32[]{:S(2)}) async-start(f32[32,32,1024]{2,1,0:T(8,128)} %copy-done.1), calls=%async_computation | async-start | bytes 8388608 | tf_op jit(solution)/shard_map/all_to_all | solution.py:366
  20.1 0.1 copy.18
  20.1 0.7 constant_dynamic-slice_fusion.cnt_ref
  20.8 0.0 copy-done.7
  20.8 0.2 dynamic-slice_reduce_fusion
  21.0 0.0 copy-done.6
  21.0 0.2 copy.16
  21.2 0.2 copy.19.tt_ref
  21.4 1.6 shard_map.65
  23.1 0.0 copy-start.2
  23.1 2.0 copy-done.2
  25.0 0.7 iota_compare_fusion.4
  25.7 0.1 select_reduce_fusion.1
  25.9 0.1 fusion.4
  26.0 0.6 pad_dynamic-slice_fusion.tmpl_ref
  26.6 89.2 %all-to-all-done = f32[32,32,1024]{2,1,0:T(8,128)} async-done(((f32[32,32,1024]{2,1,0:T(8,128)}), f32[32,32,1024]{2,1,0:T(8,128)}, u32[]{:S(2)}, u32[]{:S(2)}) %all-to-all-start) | async-done | bytes 4194336 | tf_op jit(solution)/shard_map/all_to_all | solution.py:366
  115.8 0.0 copy-start.5
  115.8 4.7 %all-to-all-start.1 = ((f32[8,32,4096]{2,1,0:T(8,128)}), f32[8,32,4096]{2,1,0:T(8,128)}, u32[]{:S(2)}, u32[]{:S(2)}) async-start(f32[8,32,4096]{2,1,0:T(8,128)} %copy-done.2), calls=%async_computation.1 | async-start | bytes 8388608 | tf_op jit(solution)/shard_map/all_to_all | solution.py:369
  120.5 0.0 copy-done.5
  120.5 67.9 %shard_map.66 = f32[32,1024]{1,0:T(8,128)S(1)} custom-call(s32[1,1]{1,0:T(1,128)} %constant_dynamic-slice_fusion.cnt_ref, f32[1024,1024]{1,0:T(8,128)} %bitcast.4.x_ref, f32[32,1024]{1,0:T(8,128)S(1)} %copy.19.tt_ref, f32[1,1024]{1,0:T(1,128)S(1)} %bitcast.24), custom_call_target="tpu_custom_call" | custom-call | flops 60000002048 | bytes 4194304 | tf_op jit(solution)/shard_map/pallas_call | solution.py:143
  188.4 0.0 all-to-all-done.1.raw_ref
  188.4 0.6 gather_fusion.1
  189.0 0.1 select_select_fusion.amp_ref
  189.1 38.2 %shard_map.67.amp_ref = f32[32,8,32,128]{3,2,1,0:T(8,128)S(1)} custom-call(f32[8,32,128]{2,1,0:T(8,128)S(1)} %select_select_fusion.amp_ref), custom_call_target="tpu_custom_call" | custom-call | tf_op jit(solution)/shard_map/pallas_call | solution.py:312
  227.3 0.0 copy-start.3
  227.3 2.0 copy-done.3
  229.3 9.8 %shard_map.68 = f32[32,256,128]{2,1,0:T(8,128)} custom-call(f32[32,32]{1,0:T(8,128)} %pad_dynamic-slice_fusion.tmpl_ref, f32[32,8,32,128]{3,2,1,0:T(8,128)} %copy-done.3, f32[8,32,4096]{2,1,0:T(8,128)} %all-to-all-done.1.raw_ref), custom_call_target="tpu_custom_call" | custom-call | tf_op jit(solution)/shard_map/pallas_call | solution.py:336
  (7 shorter events, 0.1 us)
Async XLA Ops:
  0.0 2.4 %copy-start = (s32[1,128]{1,0:T(1,128)S(1)}, s32[1,128]{1,0:T(1,128)}, u32[]{:S(2)}) copy-start(s32[1,128]{1,0:T(1,128)} %param.9) | copy-start | bytes 1540
  2.4 2.0 copy-start.8
  2.4 2.1 copy-start.4
  6.4 2.0 copy-start.1
  8.4 12.4 %copy-start.7 = (s32[1,32,8]{1,2,0:T(8,128)S(1)}, s32[1,32,8]{1,2,0:T(8,128)}, u32[]{:S(2)}) copy-start(s32[1,32,8]{1,2,0:T(8,128)} %param.11) | copy-start | bytes 3076
  8.4 12.6 %copy-start.6 = (f32[1024,30]{0,1:T(8,128)S(1)}, f32[1024,30]{0,1:T(8,128)}, u32[]{:S(2)}) copy-start(f32[1024,30]{0,1:T(8,128)} %param.7) | copy-start | bytes 368644
  8.4 107.4 %all-to-all-start = ((f32[32,32,1024]{2,1,0:T(8,128)}), f32[32,32,1024]{2,1,0:T(8,128)}, u32[]{:S(2)}, u32[]{:S(2)}) async-start(f32[32,32,1024]{2,1,0:T(8,128)} %copy-done.1), calls=%async_computation | async-start | bytes 8388608 | tf_op jit(solution)/shard_map/all_to_all | solution.py:366
  23.1 2.0 copy-start.2
  115.8 4.7 %copy-start.5 = (f32[1024]{0:T(1024)S(1)}, f32[1024]{0:T(1024)}, u32[]{:S(2)}) copy-start(f32[1024]{0:T(1024)} %param.8) | copy-start | bytes 12292
  115.8 72.6 %all-to-all-start.1 = ((f32[8,32,4096]{2,1,0:T(8,128)}), f32[8,32,4096]{2,1,0:T(8,128)}, u32[]{:S(2)}, u32[]{:S(2)}) async-start(f32[8,32,4096]{2,1,0:T(8,128)} %copy-done.2), calls=%async_computation.1 | async-start | bytes 8388608 | tf_op jit(solution)/shard_map/all_to_all | solution.py:369
  227.3 2.0 copy-start.3

commit v3 on v2

--- a/solution.py
+++ b/solution.py
@@ -235,7 +235,10 @@
     return first, events, time
 
 
-def gather_kernel(amp_ref, out_ref, own_ref, local_sem, send_sem, recv_sem, sky_send_sem, sky_recv_sem):
+def gather_kernel(amp_ref, tmpl_ref, raw_ref, out_ref, all_ref, own_ref, pix_ref, local_sem, pix_sem, send_sem, recv_sem,
+                  sky_send_sem, sky_recv_sem):
+    pixels = pltpu.make_async_copy(raw_ref, pix_ref, pix_sem)
+    pixels.start()
     chan = lax.axis_index("chan")
     sky = lax.axis_index("sky")
     slabs = amp_ref.shape[0]
@@ -260,9 +263,9 @@
         step = [0, 0]
         step[axis] = sign
         own = off == (0, 0)
-        src = own_ref.at[groups, rows] if own else out_ref.at[chunk, groups, rows]
+        src = own_ref.at[groups, rows] if own else all_ref.at[chunk, groups, rows]
         return pltpu.make_async_remote_copy(
-            src_ref=src, dst_ref=out_ref.at[chunk, groups, rows], send_sem=send_sem.at[k], recv_sem=recv_sem.at[k],
+            src_ref=src, dst_ref=all_ref.at[chunk, groups, rows], send_sem=send_sem.at[k], recv_sem=recv_sem.at[k],
             device_id={"chan": member(step)}, device_id_type=pl.DeviceIdType.MESH)
 
     barrier = pltpu.get_barrier_semaphore()
@@ -292,56 +295,56 @@
     sent = [copy(key, key[2]) for key in first]
     for c in sent:
         c.start()
-    local = pltpu.make_async_copy(own_ref, out_ref.at[chan], local_sem)
-    local.start()
+    hi, mid, low = split3(tmpl_ref[...])
+    tmpl = cat([hi, hi, mid, hi, mid, low])
+
+    def clean(part, off):
+        chunk = member(off)
+        groups = range(0, SPLIT) if part == 0 else range(SPLIT, 8)
+        amp = cat([own_ref[g] if off == (0, 0) else all_ref[chunk, g] for g in groups])
+        hi, mid, low = split3(amp)
+        model = lax.dot_general(tmpl, jnp.concatenate([low, mid, mid, hi, hi, hi], axis=0), NN_DIMS,
+                                preferred_element_type=jnp.float32)
+        at = pl.ds(pl.multiple_of(chunk * BLK, BLK), BLK)
+        for i, g in enumerate(groups):
+            rest = pix_ref[g, :, at] - model[:, i * BLK:(i + 1) * BLK]
+            out_ref[:, pl.ds(g * (RINGS[0] * RINGS[1]) + chunk, 1), :] = rest[:, None, :]
+
+    pixels.wait()
+    for part in (0, 1):
+        clean(part, (0, 0))
+    halves = set()
     for key, moved, out in events:
         copy(key, moved).wait_recv()
         for nxt in out:
             c = copy(nxt, nxt[2])
             c.start()
             sent.append(c)
-    local.wait()
+        part, axis, _, _, hop = key
+        where = (part, moved[0] % RINGS[0], moved[1] % RINGS[1])
+        if hop < RINGS[axis] // 2 or where in halves:
+            clean(part, moved)
+        halves.add(where)
     for c in sent:
         c.wait_send()
     for out, _ in swaps:
         out.wait_send()
 
 
-def gather(amp):
+def gather_clean(amp, tmpl, raw):
     count = len(gather_plan(1.0)[1])
+    owners, groups = RINGS[0] * RINGS[1], amp.shape[0]
     return pl.pallas_call(
         gather_kernel,
-        out_shape=jax.ShapeDtypeStruct((RINGS[0] * RINGS[1],) + amp.shape, jnp.float32),
-        in_specs=[pl.BlockSpec(memory_space=pltpu.VMEM)],
+        out_shape=jax.ShapeDtypeStruct((tmpl.shape[0], groups * owners, BLK), jnp.float32),
+        in_specs=[pl.BlockSpec(memory_space=pltpu.VMEM)] * 2 + [pl.BlockSpec(memory_space=pl.ANY)],
         out_specs=pl.BlockSpec(memory_space=pltpu.VMEM),
-        scratch_shapes=[pltpu.VMEM(amp.shape, jnp.float32), pltpu.SemaphoreType.DMA, pltpu.SemaphoreType.DMA((count,)),
-                        pltpu.SemaphoreType.DMA((count,)), pltpu.SemaphoreType.DMA((8,)),
-                        pltpu.SemaphoreType.DMA((8,))],
+        scratch_shapes=[pltpu.VMEM((owners,) + amp.shape, jnp.float32), pltpu.VMEM(amp.shape, jnp.float32),
+                        pltpu.VMEM(raw.shape, jnp.float32), pltpu.SemaphoreType.DMA, pltpu.SemaphoreType.DMA,
+                        pltpu.SemaphoreType.DMA((count,)), pltpu.SemaphoreType.DMA((count,)),
+                        pltpu.SemaphoreType.DMA((8,)), pltpu.SemaphoreType.DMA((8,))],
         compiler_params=pltpu.CompilerParams(collective_id=0, has_side_effects=True, vmem_limit_bytes=40 << 20),
-    )(amp)
-
-
-def clean_kernel(tmpl_ref, amp_ref, raw_ref, out_ref):
-    owners = amp_ref.shape[0]
-    for c in range(0, owners, 8):
-        amp = jnp.concatenate([amp_ref[c + i, 0] for i in range(8)], axis=1)
-        rest = raw_ref[0, :, c * BLK:(c + 8) * BLK] - mm_nn(tmpl_ref[...], amp)
-        for i in range(8):
-            out_ref[:, c + i, :] = rest[:, i * BLK:(i + 1) * BLK]
-
-
-def clean(tmpl, amp, raw):
-    owners, groups = amp.shape[0], amp.shape[1]
-    rows = raw.shape[1]
-    return pl.pallas_call(
-        clean_kernel,
-        grid=(groups,),
-        out_shape=jax.ShapeDtypeStruct((rows, groups * owners, BLK), jnp.float32),
-        in_specs=[pl.BlockSpec(tmpl.shape, lambda g: (0, 0)),
-                  pl.BlockSpec((owners, 1, amp.shape[2], BLK), lambda g: (0, g, 0, 0)),
-                  pl.BlockSpec((1, rows, owners * BLK), lambda g: (g, 0, 0))],
-        out_specs=pl.BlockSpec((rows, owners, BLK), lambda g: (0, g, 0)),
-    )(tmpl, amp, raw)
+    )(amp, tmpl, raw)
 
 
 def tables(order_row, counts_row, dest_rows, slabs):
@@ -377,9 +380,8 @@
     source = jnp.sum(jnp.where(match, slot_index[None, :], 0), axis=1)
     amp = jnp.take(amp.reshape(32, CAP, BLK).transpose(1, 0, 2), source, axis=0)
     amp = jnp.where(jnp.any(match, axis=1)[:, None, None], amp, 0.0)
-    amp = gather(amp)
     own = lax.dynamic_slice_in_dim(padded, member * rows, rows, 0)
-    return clean(own, amp, raw)
+    return gather_clean(amp, own, raw)
 
 
 def solution(mesh):

time: 240 us -> 231 us (0.963)
  Pallas kernels: 119 us -> 111 us
    pallas_call x2 -> x1, Pallas kernels: 48 us -> 39.4 us  [gather_clean(): pl.pallas_call(gather_kernel, out_shape=jax.ShapeDtypeStruct((tmpl.shape[...]
    unnamed x19 -> x18, local copies, waits for them, and re-layouts: 6.18 us -> 6.23 us
  transfers between devices with their start and end apart: 2 -> 2, of which waited for: 1 -> 1; matrix products, arithmetic and copies ran while one was open for 1% -> 1% of each run, Pallas kernels for 29% -> 30%
where the time goes in v3:
time: 231 us; the launch traced here: 230 us
  Pallas kernels  111 us (48%)
  waiting for transfers between devices  89.9 us (39%)
  starting transfers between devices  16.3 us (7%)
  local copies, waits for them, and re-layouts  10.7 us (5%)
  other arithmetic  2.63 us (1%)
    all_to_all x1, waiting for transfers between devices, on_device(): lax.all_to_all(outgoing, 'chan', split_axis=0, concat_axis=0, tiled=True)  89.9 us
    pallas_call x1, Pallas kernels, gls(): pl.pallas_call(functools.partial(gls_kernel, nb=nb), out_shape=jax.ShapeD...  67.9 us
    pallas_call x1, Pallas kernels, gather_clean(): pl.pallas_call(gather_kernel, out_shape=jax.ShapeDtypeStruct((tmpl.shape[...  39.4 us
    all_to_all x1, starting transfers between devices, on_device(): lax.all_to_all(outgoing, 'chan', split_axis=0, concat_axis=0, tiled=True)  11.7 us
    unnamed x18, local copies, waits for them, and re-layouts  6.23 us
    all_to_all x1, starting transfers between devices, on_device(): lax.all_to_all(sky_out, 'sky', split_axis=0, concat_axis=0, tiled=True)  4.68 us
  transfers between devices with their start and end apart: 2, of which 1 were waited for; matrix products, arithmetic and copies ran while one was open for 1% of the time, Pallas kernels for 30%

profile of v3, /device:TPU:24, one launch (start us, length us, event | category | flops | bytes accessed | tf_op | source)
XLA Modules:
  0.0 230.4 jit_solution(2192421034310590687)
XLA Ops:
  0.0 0.0 copy-start
  0.0 0.7 copy.16
  0.8 0.1 reduce-window.8
  0.8 0.1 reduce.1
  0.9 0.7 bitcast_subtract_fusion
  1.6 0.7 compare_select_fusion
  2.3 0.1 reshape.232
  2.4 0.0 copy-done
  2.4 0.0 copy-start.7
  2.4 0.0 copy-start.3
  2.5 1.9 gather_fusion
  4.3 0.1 reshape.231
  4.4 0.0 copy-done.7
  4.4 0.1 select_select_fusion.1.slot_ref
  4.5 0.0 copy-done.3
  4.5 1.8 shard_map.64
  6.4 0.0 copy-start.1
  6.4 2.0 copy-done.1
  8.4 0.0 copy-start.6
  8.4 0.0 copy-start.5
  8.4 11.7 %all-to-all-start = ((f32[32,32,1024]{2,1,0:T(8,128)}), f32[32,32,1024]{2,1,0:T(8,128)}, u32[]{:S(2)}, u32[]{:S(2)}) async-start(f32[32,32,1024]{2,1,0:T(8,128)} %copy-done.1), calls=%async_computation | async-start | bytes 8388608 | tf_op jit(solution)/shard_map/all_to_all | solution.py:369
  20.1 0.1 copy.17
  20.1 0.6 constant_dynamic-slice_fusion.cnt_ref
  20.7 0.0 copy-done.6
  20.7 0.2 dynamic-slice_reduce_fusion
  20.9 0.0 copy-done.5
  20.9 0.2 copy.18
  21.2 0.2 copy.19.tt_ref
  21.4 1.6 shard_map.65
  23.0 0.0 copy-start.2
  23.0 2.0 copy-done.2
  25.0 0.6 iota_compare_fusion.4
  25.6 0.1 select_reduce_fusion.1
  25.8 0.1 fusion.4
  25.9 89.9 %all-to-all-done = f32[32,32,1024]{2,1,0:T(8,128)} async-done(((f32[32,32,1024]{2,1,0:T(8,128)}), f32[32,32,1024]{2,1,0:T(8,128)}, u32[]{:S(2)}, u32[]{:S(2)}) %all-to-all-start) | async-done | bytes 4194336 | tf_op jit(solution)/shard_map/all_to_all | solution.py:369
  115.8 0.0 copy-start.4
  115.8 4.7 %all-to-all-start.1 = ((f32[8,32,4096]{2,1,0:T(8,128)}), f32[8,32,4096]{2,1,0:T(8,128)}, u32[]{:S(2)}, u32[]{:S(2)}) async-start(f32[8,32,4096]{2,1,0:T(8,128)} %copy-done.2), calls=%async_computation.1 | async-start | bytes 8388608 | tf_op jit(solution)/shard_map/all_to_all | solution.py:372
  120.5 0.0 copy-done.4
  120.5 67.9 %shard_map.66 = f32[32,1024]{1,0:T(8,128)S(1)} custom-call(s32[1,1]{1,0:T(1,128)} %constant_dynamic-slice_fusion.cnt_ref, f32[1024,1024]{1,0:T(8,128)} %bitcast.4.x_ref, f32[32,1024]{1,0:T(8,128)S(1)} %copy.19.tt_ref, f32[1,1024]{1,0:T(1,128)S(1)} %bitcast.24), custom_call_target="tpu_custom_call" | custom-call | flops 60000002048 | bytes 4194304 | tf_op jit(solution)/shard_map/pallas_call | solution.py:143
  188.3 0.0 all-to-all-done.1.raw_ref
  188.4 0.6 gather_fusion.1
  188.9 0.1 select_select_fusion.amp_ref
  189.0 39.4 %shard_map.67 = f32[32,256,128]{2,1,0:T(8,128)S(1)} custom-call(f32[8,32,128]{2,1,0:T(8,128)S(1)} %select_select_fusion.amp_ref, f32[32,32]{1,0:T(8,128)S(1)} %pad_dynamic-slice_fusion.tmpl_ref, f32[8,32,4096]{2,1,0:T(8,128)} %all-to-all-done.1.raw_ref), custom_call_target="tpu_custom_call" | custom-call | tf_op jit(solution)/shard_map/pallas_call | solution.py:337
  228.4 2.0 copy.24
  (8 shorter events, 0.1 us)
Async XLA Ops:
  0.0 2.4 %copy-start = (s32[1,128]{1,0:T(1,128)S(1)}, s32[1,128]{1,0:T(1,128)}, u32[]{:S(2)}) copy-start(s32[1,128]{1,0:T(1,128)} %param.9) | copy-start | bytes 1540
  2.4 2.0 copy-start.7
  2.4 2.1 copy-start.3
  6.4 2.0 copy-start.1
  8.4 12.4 %copy-start.6 = (s32[1,32,8]{1,2,0:T(8,128)S(1)}, s32[1,32,8]{1,2,0:T(8,128)}, u32[]{:S(2)}) copy-start(s32[1,32,8]{1,2,0:T(8,128)} %param.11) | copy-start | bytes 3076
  8.4 12.5 %copy-start.5 = (f32[1024,30]{0,1:T(8,128)S(1)}, f32[1024,30]{0,1:T(8,128)}, u32[]{:S(2)}) copy-start(f32[1024,30]{0,1:T(8,128)} %param.7) | copy-start | bytes 368644
  8.4 107.4 %all-to-all-start = ((f32[32,32,1024]{2,1,0:T(8,128)}), f32[32,32,1024]{2,1,0:T(8,128)}, u32[]{:S(2)}, u32[]{:S(2)}) async-start(f32[32,32,1024]{2,1,0:T(8,128)} %copy-done.1), calls=%async_computation | async-start | bytes 8388608 | tf_op jit(solution)/shard_map/all_to_all | solution.py:369
  23.0 2.0 copy-start.2
  115.8 4.7 %copy-start.4 = (f32[1024]{0:T(1024)S(1)}, f32[1024]{0:T(1024)}, u32[]{:S(2)}) copy-start(f32[1024]{0:T(1024)} %param.8) | copy-start | bytes 12292
  115.8 72.6 %all-to-all-start.1 = ((f32[8,32,4096]{2,1,0:T(8,128)}), f32[8,32,4096]{2,1,0:T(8,128)}, u32[]{:S(2)}, u32[]{:S(2)}) async-start(f32[8,32,4096]{2,1,0:T(8,128)} %copy-done.2), calls=%async_computation.1 | async-start | bytes 8388608 | tf_op jit(solution)/shard_map/all_to_all | solution.py:372

commit v4 on v3

--- a/solution.py
+++ b/solution.py
@@ -155,14 +155,17 @@
 
 
 def slot_kernel(slot_ref, map_ref, out_ref):
+    owners = out_ref.shape[0]
+    base = pl.program_id(0) * owners
+
     def put(c, carry):
         for j in range(CAP):
-            block = slot_ref[c, j]
+            block = slot_ref[base + c, j]
             at = pl.multiple_of(jnp.maximum(block, 0) * BLK, BLK)
             tile = map_ref[:, pl.ds(at, BLK)]
             out_ref[c, :, j * BLK:(j + 1) * BLK] = jnp.where(block >= 0, tile, 0.0)
         return carry
-    lax.fori_loop(0, slot_ref.shape[0], put, 0)
+    lax.fori_loop(0, owners, put, 0)
 
 
 def slab_kernel(slab_ref, map_ref, out_ref):
@@ -177,12 +180,13 @@
     lax.fori_loop(0, slab_ref.shape[1], put, 0)
 
 
-def pack(kernel, blocks, shape, sky_map):
+def pack(kernel, blocks, shape, sky_map, steps=1):
     return pl.pallas_call(
         kernel,
-        out_shape=jax.ShapeDtypeStruct(shape, jnp.float32),
+        grid=(steps,),
+        out_shape=pltpu.MemorySpace.HBM(shape, jnp.float32),
         in_specs=[pl.BlockSpec(memory_space=pltpu.SMEM), pl.BlockSpec(memory_space=pltpu.VMEM)],
-        out_specs=pl.BlockSpec(memory_space=pltpu.VMEM),
+        out_specs=pl.BlockSpec((shape[0] // steps,) + shape[1:], lambda g: (g, 0, 0)),
         cost_estimate=pl.CostEstimate(flops=10**6, bytes_accessed=6 << 20, transcendentals=0),
         compiler_params=pltpu.CompilerParams(vmem_limit_bytes=40 << 20),
     )(blocks, sky_map)
@@ -364,7 +368,7 @@
     rows = sky_map.shape[0]
     slot_block, slab_block = tables(block_order[0], patch_count[0], slab_dest[0], slabs)
     owners = slot_block.shape[0]
-    outgoing = pack(slot_kernel, slot_block, (owners, rows, CAP * BLK), sky_map)
+    outgoing = pack(slot_kernel, slot_block, (owners, rows, CAP * BLK), sky_map, steps=8)
     sky_out = pack(slab_kernel, slab_block, (slabs, rows, owners * BLK), sky_map)
     pixels = lax.all_to_all(outgoing, "chan", split_axis=0, concat_axis=0, tiled=True)
     pixels = pixels.reshape(NU, CAP * BLK)

time: 231 us -> 232 us (level)
  Pallas kernels: 111 us -> 116 us
  local copies, waits for them, and re-layouts: 10.7 us -> 6.69 us
    pallas_call x2, Pallas kernels: 3.46 us -> 8.37 us  [pack(): pl.pallas_call(kernel, grid=(steps,), out_shape=pltpu.MemorySpace.HBM(sha...]
    unnamed x18 -> x14, local copies, waits for them, and re-layouts: 6.23 us -> 2.26 us
  transfers between devices with their start and end apart: 2 -> 2, of which waited for: 1 -> 1; matrix products, arithmetic and copies ran while one was open for 1% -> 1% of each run, Pallas kernels for 30% -> 31%
where the time goes in v4:
time: 232 us; the launch traced here: 231 us
  Pallas kernels  116 us (50%)
  waiting for transfers between devices  89.9 us (39%)
  starting transfers between devices  16.3 us (7%)
  local copies, waits for them, and re-layouts  6.69 us (3%)
  other arithmetic  2.63 us (1%)
    all_to_all x1, waiting for transfers between devices, on_device(): lax.all_to_all(outgoing, 'chan', split_axis=0, concat_axis=0, tiled=True)  89.9 us
    pallas_call x1, Pallas kernels, gls(): pl.pallas_call(functools.partial(gls_kernel, nb=nb), out_shape=jax.ShapeD...  67.9 us
    pallas_call x1, Pallas kernels, gather_clean(): pl.pallas_call(gather_kernel, out_shape=jax.ShapeDtypeStruct((tmpl.shape[...  39.4 us
    all_to_all x1, starting transfers between devices, on_device(): lax.all_to_all(outgoing, 'chan', split_axis=0, concat_axis=0, tiled=True)  11.7 us
    pallas_call x2, Pallas kernels, pack(): pl.pallas_call(kernel, grid=(steps,), out_shape=pltpu.MemorySpace.HBM(sha...  8.37 us
    all_to_all x1, starting transfers between devices, on_device(): lax.all_to_all(sky_out, 'sky', split_axis=0, concat_axis=0, tiled=True)  4.68 us
  transfers between devices with their start and end apart: 2, of which 1 were waited for; matrix products, arithmetic and copies ran while one was open for 1% of the time, Pallas kernels for 31%

profile of v4, /device:TPU:24, one launch (start us, length us, event | category | flops | bytes accessed | tf_op | source)
XLA Modules:
  0.0 231.3 jit_solution(13012417495780211422)
XLA Ops:
  0.0 0.0 copy-start
  0.0 0.7 copy.16
  0.8 0.1 reduce-window.8
  0.8 0.1 reduce.1
  0.9 0.7 bitcast_subtract_fusion
  1.6 0.7 compare_select_fusion
  2.3 0.1 reshape.232
  2.4 0.0 copy-done
  2.4 0.0 copy-start.5
  2.4 0.0 copy-start.1
  2.5 1.9 gather_fusion
  4.3 0.1 reshape.231
  4.4 0.0 copy-done.5
  4.4 0.1 select_select_fusion.1.slot_ref
  4.5 0.0 copy-done.1
  4.5 4.7 %shard_map.64 = f32[32,32,1024]{2,1,0:T(8,128)} custom-call(s32[32,8]{1,0:T(8,128)S(1)} %select_select_fusion.1.slot_ref, f32[32,16384]{1,0:T(8,128)S(1)} %copy-done.1), custom_call_target="tpu_custom_call" | custom-call | flops 1000000 | bytes 6291456 | tf_op jit(solution)/shard_map/pallas_call | solution.py:184
  9.3 0.0 copy-start.4
  9.3 0.0 copy-start.3
  9.3 11.7 %all-to-all-start = ((f32[32,32,1024]{2,1,0:T(8,128)}), f32[32,32,1024]{2,1,0:T(8,128)}, u32[]{:S(2)}, u32[]{:S(2)}) async-start(f32[32,32,1024]{2,1,0:T(8,128)} %shard_map.64), calls=%async_computation | async-start | bytes 8388608 | tf_op jit(solution)/shard_map/all_to_all | solution.py:373
  20.9 0.1 copy.17
  21.0 0.6 constant_dynamic-slice_fusion.cnt_ref
  21.6 0.0 copy-done.4
  21.6 0.2 dynamic-slice_reduce_fusion
  21.8 0.0 copy-done.3
  21.8 0.2 copy.18
  22.1 0.2 copy.19.tt_ref
  22.3 3.6 %shard_map.65 = f32[8,32,4096]{2,1,0:T(8,128)} custom-call(s32[8,32]{1,0:T(8,128)S(1)} %select_reduce_fusion.slab_ref, f32[32,16384]{1,0:T(8,128)S(1)} %copy-done.1), custom_call_target="tpu_custom_call" | custom-call | flops 1000000 | bytes 6291456 | tf_op jit(solution)/shard_map/pallas_call | solution.py:184
  25.9 0.6 iota_compare_fusion.4
  26.5 0.1 select_reduce_fusion.1
  26.7 0.1 fusion.4
  26.8 89.9 %all-to-all-done = f32[32,32,1024]{2,1,0:T(8,128)} async-done(((f32[32,32,1024]{2,1,0:T(8,128)}), f32[32,32,1024]{2,1,0:T(8,128)}, u32[]{:S(2)}, u32[]{:S(2)}) %all-to-all-start) | async-done | bytes 4194336 | tf_op jit(solution)/shard_map/all_to_all | solution.py:373
  116.7 0.0 copy-start.2
  116.7 4.7 %all-to-all-start.1 = ((f32[8,32,4096]{2,1,0:T(8,128)}), f32[8,32,4096]{2,1,0:T(8,128)}, u32[]{:S(2)}, u32[]{:S(2)}) async-start(f32[8,32,4096]{2,1,0:T(8,128)} %shard_map.65), calls=%async_computation.1 | async-start | bytes 8388608 | tf_op jit(solution)/shard_map/all_to_all | solution.py:376
  121.4 0.0 copy-done.2
  121.4 67.9 %shard_map.66 = f32[32,1024]{1,0:T(8,128)S(1)} custom-call(s32[1,1]{1,0:T(1,128)} %constant_dynamic-slice_fusion.cnt_ref, f32[1024,1024]{1,0:T(8,128)} %bitcast.4.x_ref, f32[32,1024]{1,0:T(8,128)S(1)} %copy.19.tt_ref, f32[1,1024]{1,0:T(1,128)S(1)} %bitcast.24), custom_call_target="tpu_custom_call" | custom-call | flops 60000002048 | bytes 4194304 | tf_op jit(solution)/shard_map/pallas_call | solution.py:143
  189.2 0.0 all-to-all-done.1.raw_ref
  189.3 0.6 gather_fusion.1
  189.8 0.1 select_select_fusion.amp_ref
  189.9 39.4 %shard_map.67 = f32[32,256,128]{2,1,0:T(8,128)S(1)} custom-call(f32[8,32,128]{2,1,0:T(8,128)S(1)} %select_select_fusion.amp_ref, f32[32,32]{1,0:T(8,128)S(1)} %pad_dynamic-slice_fusion.tmpl_ref, f32[8,32,4096]{2,1,0:T(8,128)} %all-to-all-done.1.raw_ref), custom_call_target="tpu_custom_call" | custom-call | tf_op jit(solution)/shard_map/pallas_call | solution.py:341
  229.3 2.0 copy.24
  (8 shorter events, 0.1 us)
Async XLA Ops:
  0.0 2.4 %copy-start = (s32[1,128]{1,0:T(1,128)S(1)}, s32[1,128]{1,0:T(1,128)}, u32[]{:S(2)}) copy-start(s32[1,128]{1,0:T(1,128)} %param.9) | copy-start | bytes 1540
  2.4 2.0 copy-start.5
  2.4 2.1 copy-start.1
  9.3 12.4 %copy-start.4 = (s32[1,32,8]{1,2,0:T(8,128)S(1)}, s32[1,32,8]{1,2,0:T(8,128)}, u32[]{:S(2)}) copy-start(s32[1,32,8]{1,2,0:T(8,128)} %param.11) | copy-start | bytes 3076
  9.3 12.5 %copy-start.3 = (f32[1024,30]{0,1:T(8,128)S(1)}, f32[1024,30]{0,1:T(8,128)}, u32[]{:S(2)}) copy-start(f32[1024,30]{0,1:T(8,128)} %param.7) | copy-start | bytes 368644
  9.3 107.4 %all-to-all-start = ((f32[32,32,1024]{2,1,0:T(8,128)}), f32[32,32,1024]{2,1,0:T(8,128)}, u32[]{:S(2)}, u32[]{:S(2)}) async-start(f32[32,32,1024]{2,1,0:T(8,128)} %shard_map.64), calls=%async_computation | async-start | bytes 8388608 | tf_op jit(solution)/shard_map/all_to_all | solution.py:373
  116.7 4.7 %copy-start.2 = (f32[1024]{0:T(1024)S(1)}, f32[1024]{0:T(1024)}, u32[]{:S(2)}) copy-start(f32[1024]{0:T(1024)} %param.8) | copy-start | bytes 12292
  116.7 72.6 %all-to-all-start.1 = ((f32[8,32,4096]{2,1,0:T(8,128)}), f32[8,32,4096]{2,1,0:T(8,128)}, u32[]{:S(2)}, u32[]{:S(2)}) async-start(f32[8,32,4096]{2,1,0:T(8,128)} %shard_map.65), calls=%async_computation.1 | async-start | bytes 8388608 | tf_op jit(solution)/shard_map/all_to_all | solution.py:376
